TPU v7x, 32 devices: a whole 2x2x4 slice. The times are simulated.
32 devices in a mesh: elem: 16 (over z, x, core), section: 2 (over y).
Axes of the slice: x: 2, y: 2, z: 4, core: 2. Of those that a mesh axis runs over, the one named last changes fastest.
Arguments:
- u_start: float32 [512, 320], P('elem'), may hold values from -6 to 6
- inverses: float32 [512, 320, 320], P('elem'), may hold values from -1 to 2
- neighbours: int32 [512, 5], P('elem'), may hold values from 0 to 511, as said below
- partners: int32 [512], replicated, may hold values from 0 to 511, as said below
Outputs:
- section_states: float32 [4, 512, 320], P('section', 'elem')
Inputs may be any that keep to these rules, and one draw needn't show every extreme that they name: `neighbours`: every entry names an element on the same device as the row's element, or on the device just before or after it along elem, cyclically. The partners of the 32 elements of device d along elem lie on devices d + 4 and d + 5, cyclically, 16 on each.
All inputs are finite; a program needn't handle non-finite values.
Results may differ from a plain program's by a relative error of at most 0.0001.
Values sent between devices are 32-bit elements; how exact they have to be, the bound alone decides.
A program may use at most 64 MiB of HBM per device.

v0:
```python
import functools
import math

import jax
import jax.numpy as jnp
from jax import lax
from jax.experimental import pallas as pl
from jax.experimental.pallas import tpu as pltpu
from jax.sharding import PartitionSpec as P

NODE1 = 4
SECTIONS = 4
NEWTON = 2


time_step = 0.03
dissipation = 2.0
enthalpy_factor = 3.5
radau_nodes = [0.08858795951270394, 0.4094668644407347, 0.787659461760847, 1.0]


def lobatto():
    node_count = NODE1
    inner_value = 1.0 / math.sqrt(5.0)
    lobatto_nodes = [-1.0, -inner_value, inner_value, 1.0]
    products = []
    for row in range(node_count):
        value = 1.0
        for other in range(node_count):
            if other != row:
                value = value * (lobatto_nodes[row] - lobatto_nodes[other])
        products.append(value)
    derivative = []
    for row in range(node_count):
        entries = []
        for column in range(node_count):
            if row == column:
                total = 0.0
                for other in range(node_count):
                    if other != row:
                        total = total + 1.0 / (lobatto_nodes[row] - lobatto_nodes[other])
                entries.append(2.0 * total)
            else:
                entries.append(
                    2.0
                    * (products[row] / products[column])
                    / (lobatto_nodes[row] - lobatto_nodes[column])
                )
        derivative.append(entries)
    return derivative, float(node_count * (node_count - 1) / 2.0)


def radau_table():
    section_total = SECTIONS
    butcher = []
    columns = []
    for column in range(section_total):
        coeffs = [1.0]
        scale = 1.0
        for other in range(section_total):
            if other != column:
                shifted = [0.0] + coeffs
                for position in range(len(coeffs)):
                    shifted[position] = shifted[position] - radau_nodes[other] * coeffs[position]
                coeffs = shifted
                scale = scale * (radau_nodes[column] - radau_nodes[other])
        integral = [0.0] + [
            coeffs[position] / (position + 1.0) / scale for position in range(len(coeffs))
        ]
        columns.append(integral)
    for row in range(section_total):
        entries = []
        for column in range(section_total):
            value = 0.0
            for coefficient in reversed(columns[column]):
                value = value * radau_nodes[row] + coefficient
            entries.append(value)
        butcher.append(entries)
    return butcher


FIELDS = 5
NODES = NODE1**3
FACE = NODE1**2
LANES = 128
GROUP = 8
ROWS = 64
MESH = pl.DeviceIdType.MESH


def strided(start, count):
    return pl.ds(start, count, stride=NODE1)


def to_k_order(src_ref, k_ref):
    for field in range(FIELDS):
        for k in range(NODE1):
            base = field * NODES
            k_ref[base + k * FACE : base + (k + 1) * FACE, :] = src_ref[strided(base + k, FACE), :]


def slab(src_ref, k_ref, direction, position):
    out = []
    for field in range(FIELDS):
        base = field * NODES
        if direction == 0:
            out.append(src_ref[base + position * FACE : base + (position + 1) * FACE, :])
        elif direction == 1:
            out.append(k_ref[strided(base + position, FACE), :])
        else:
            out.append(k_ref[base + position * FACE : base + (position + 1) * FACE, :])
    return out


def put_slabs(out_ref, k_ref, direction, slabs):
    for position in range(NODE1):
        for field in range(FIELDS):
            base = field * NODES
            rows = slice(base + position * FACE, base + (position + 1) * FACE)
            value = slabs[position][field]
            if direction == 0:
                out_ref[rows, :] = value
            elif direction == 1:
                k_ref[strided(base + position, FACE), :] = value
            else:
                value = k_ref[rows, :] + value
                there = strided(base + position, FACE)
                out_ref[there, :] = out_ref[there, :] + value


def speed2(state):
    return state[1] * state[1] + state[2] * state[2] + state[3] * state[3]


def two_point(a, ka, b, kb, direction):
    r = a[0] + b[0]
    v = [a[1 + c] + b[1 + c] for c in range(3)]
    p = a[4] + b[4]
    n = v[direction]
    m = (0.25 * r) * n
    half = 0.5 * m
    out = [m]
    for c in range(3):
        term = half * v[c]
        if c == direction:
            term = term + 0.5 * p
        out.append(term)
    out.append((0.25 * enthalpy_factor * p) * n + (0.5 * half) * (ka + kb))
    return out


def tendency(uc, uk, faces, out_ref, tk, scale):
    deriv, inv_weight = lobatto()
    for direction in range(3):
        states = [slab(uc, uk, direction, pos) for pos in range(NODE1)]
        speeds = [speed2(state) for state in states]
        sums = [None] * NODE1
        for a in range(NODE1):
            for b in range(a + 1, NODE1):
                f = two_point(states[a], speeds[a], states[b], speeds[b], direction)
                for at, other in ((a, b), (b, a)):
                    c = -2.0 * scale * deriv[at][other]
                    terms = [c * x for x in f]
                    sums[at] = terms if sums[at] is None else [x + y for x, y in zip(sums[at], terms)]
        for upper in range(2):
            pos = (NODE1 - 1) * upper
            sign = 2.0 * upper - 1.0
            other = faces(2 * direction + upper)
            f = two_point(states[pos], speeds[pos], other, speed2(other), direction)
            c = -2.0 * scale * inv_weight
            d = 0.5 * dissipation * c
            sums[pos] = [
                total + (c * sign) * x - d * (n - u)
                for total, x, n, u in zip(sums[pos], f, other, states[pos])
            ]
        put_slabs(out_ref, tk, direction, sums)


def lift(faces, out_ref, tk):
    zero = jnp.zeros((FACE, LANES), jnp.float32)
    for direction in range(3):
        slabs = [[zero] * FIELDS for _ in range(NODE1)]
        slabs[0] = faces(2 * direction)
        slabs[NODE1 - 1] = faces(2 * direction + 1)
        put_slabs(out_ref, tk, direction, slabs)


def kernel(
    devices, count, u_ref, nbr_ref, inv_ref, out_ref,
    a_ref, recv_ref, zrecv_ref, zsend_ref, pick_ref, near_ref,
    uc, uk, vc, wc, lc, tk, nc, nk, fc, gc, xr,
    a_sem, send_sem, recv_sem,
):
    rank = lax.axis_index("elem")
    part = lax.axis_index("section")
    parts = lax.axis_size("section")
    own_sections = SECTIONS // parts
    rotation = devices // 4
    unknowns = FIELDS * NODES
    butcher = radau_table()
    _, inv_weight = lobatto()
    groups = count // GROUP

    def at(offset):
        return lax.rem(rank + (offset + devices), devices)

    def load(g):
        block = pl.ds(g * GROUP, GROUP)
        return pltpu.make_async_copy(inv_ref.at[block], a_ref.at[block], a_sem.at[g])

    for g in range(groups):
        load(g).start()

    barrier = pltpu.get_barrier_semaphore()
    others = (1, -1, rotation, -rotation, rotation + 1, -rotation - 1)
    for offset in others:
        pl.semaphore_signal(barrier, inc=1, device_id={"elem": at(offset)}, device_id_type=MESH)
    pl.semaphore_wait(barrier, len(others))

    def copy(x, which):
        if which < 2:
            src = u_ref if x == 0 else recv_ref.at[x, pl.ds(2 * count, count)]
            dst = recv_ref.at[x, pl.ds(which * count, count)]
            target = at(1) if which == 0 else at(-1)
        else:
            src = zsend_ref.at[x]
            dst = zrecv_ref.at[x, pl.ds((which - 2) * count, count)]
            target = at(-rotation) if which == 2 else at(-rotation - 1)
        return pltpu.make_async_remote_copy(
            src_ref=src, dst_ref=dst, send_sem=send_sem.at[x, which],
            recv_sem=recv_sem.at[x, which], device_id={"elem": target}, device_id_type=MESH,
        )

    copy(0, 0).start()
    copy(0, 1).start()

    def lower_rows(col_ref):
        low = col_ref[strided(0, FIELDS * FACE), :]
        low = jnp.concatenate([low, jnp.zeros((LANES - FIELDS * FACE, LANES), jnp.float32)], axis=0)
        return low.T

    def send(x, col_ref, vectors):
        low = lower_rows(col_ref)
        for s in range(vectors):
            zsend_ref[x + s] = low[s * count : (s + 1) * count]
        for s in range(vectors):
            copy(x + s, 2).start()
            copy(x + s, 3).start()
        rows = col_ref[...].T
        for s in range(vectors):
            recv_ref[x + s, 2 * count : 3 * count] = rows[s * count : (s + 1) * count]
        for s in range(vectors):
            copy(x + s, 0).start()
            copy(x + s, 1).start()

    u_rows = u_ref[...]
    recv_ref[0, 2 * count : 3 * count] = u_rows
    uc[...] = jnp.concatenate([u_rows] * SECTIONS, axis=0).T
    zsend_ref[0] = lower_rows(uc)[:count]
    copy(0, 2).start()
    copy(0, 3).start()
    to_k_order(uc, uk)

    lane = lax.broadcasted_iota(jnp.int32, (1, LANES), 1)
    block = lane // count
    local = lane - block * count

    def ids(*offsets):
        out = jnp.full((1, LANES), -1, jnp.int32)
        for index, offset in enumerate(offsets):
            out = jnp.where(block == index, at(offset) * count + local, out)
        return out

    side_ids = ids(-1, 1, 0)
    sliding_ids = ids(rotation, rotation + 1)
    for face in range(6):
        match = nbr_ref[:, face : face + 1] == (side_ids if face < 5 else sliding_ids)
        match = jnp.where(match, 1.0, 0.0)
        pick_ref[face] = jnp.concatenate([match] * SECTIONS, axis=0).astype(jnp.bfloat16)

    def picked(face, values):
        high = values.astype(jnp.bfloat16)
        rest = values - high.astype(jnp.float32)
        middle = rest.astype(jnp.bfloat16)
        low = (rest - middle.astype(jnp.float32)).astype(jnp.bfloat16)
        split = jnp.concatenate([high, middle, low], axis=0)
        got = lax.dot_general(
            split, pick_ref[face], (((1,), (1,)), ((), ())), preferred_element_type=jnp.float32
        )
        n = values.shape[0]
        return (got[2 * n :] + got[n : 2 * n]) + got[:n]

    def receive(x, put):
        for which in range(4):
            copy(x, which).wait_recv()
        mine = recv_ref[x]
        nc[...] = jnp.concatenate([mine, mine[2 * count :]], axis=0).T
        to_k_order(nc, nk)
        for face in range(5):
            position = (NODE1 - 1) * (1 - face % 2)
            put(face, picked(face, jnp.concatenate(slab(nc, nk, face // 2, position), axis=0)))
        sliding = zrecv_ref[x]
        sliding = jnp.concatenate([sliding, sliding], axis=0).T
        put(5, picked(5, sliding[: FIELDS * FACE]))

    def keep(slot):
        def put(face, value):
            near_ref[slot, face] = value
        return put

    def near(slot):
        def faces(face):
            return [near_ref[slot, face, f * FACE : (f + 1) * FACE, :] for f in range(FIELDS)]
        return faces

    def per_lane(value_of):
        out = jnp.zeros((1, LANES), jnp.float32)
        for group in range(SECTIONS):
            value = jnp.float32(value_of(0, group))
            for other in range(1, parts):
                value = jnp.where(part == other, jnp.float32(value_of(other, group)), value)
            out = jnp.where(block == group, value, out)
        return out

    def matvec(dst, vectors, first):
        dst[...] = jnp.zeros_like(dst)

        @pl.loop(0, groups)
        def _(g):
            if first:
                load(g).wait()
            xs = [
                xr[pl.ds(pl.multiple_of(s * count + g * GROUP, GROUP), GROUP), :]
                for s in range(vectors)
            ]

            @pl.loop(0, unknowns // ROWS)
            def _(c):
                rows = pl.ds(pl.multiple_of(c * ROWS, ROWS), ROWS)
                acc = dst[rows, :]
                for k in range(GROUP):
                    e = g * GROUP + k
                    a = a_ref[e, rows, :]
                    for s in range(vectors):
                        total = jnp.sum(a * xs[s][k : k + 1, :], axis=1, keepdims=True)
                        where = local == e if vectors == 1 else lane == s * count + e
                        acc = jnp.where(where, total, acc)
                dst[rows, :] = acc

    receive(0, keep(0))
    tendency(uc, uk, near(0), lc, tk, 1.0)
    xr[...] = lc[...].T
    matvec(vc, 1, True)
    send(1, vc, 1)
    receive(1, keep(1))
    lift(near(1), lc, tk)
    xr[...] = lc[...].T
    matvec(wc, 1, False)
    send(2, wc, 1)

    def alpha(i):
        return time_step * sum(butcher[i])

    def coupling(i):
        return time_step * butcher[i][i] * dissipation * inv_weight

    def own(p, group):
        return p * own_sections + group % own_sections

    alphas = per_lane(lambda p, s: alpha(s))
    betas = per_lane(lambda p, s: alpha(s) * coupling(s))
    gc[...] = uc[...] + alphas * vc[...] + betas * wc[...]
    to_k_order(gc, uk)

    def add(face, value):
        near_ref[0, face] = near_ref[0, face] + alphas * near_ref[1, face] + betas * value

    receive(2, add)
    tendency(gc, uk, near(0), lc, tk, time_step)

    own_alphas = per_lane(lambda p, g: alpha(own(p, g)))
    own_betas = per_lane(lambda p, g: alpha(own(p, g)) * coupling(own(p, g)))
    own_couplings = per_lane(lambda p, g: coupling(own(p, g)))
    step = own_alphas * vc[...] + own_betas * wc[...]
    tend = lc[...]
    total = -step
    for shift in range(SECTIONS):
        moved = tend if shift == 0 else pltpu.roll(tend, shift * count, 1)
        weights = per_lane(lambda p, g: butcher[own(p, g)][(g - shift) % SECTIONS])
        total = total + weights * moved
    gc[...] = uc[...] + step
    xr[...] = total.T
    matvec(fc, own_sections, False)
    send(3, fc, own_sections)
    receive(3, keep(0))
    for s in range(1, own_sections):
        def merge(face, value, s=s):
            near_ref[0, face] = jnp.where(block == s, value, near_ref[0, face])
        receive(3 + s, merge)
    lift(near(0), lc, tk)
    xr[...] = (own_couplings * lc[...]).T
    matvec(wc, own_sections, False)
    rows = (gc[...] + fc[...] + wc[...]).T
    for s in range(own_sections):
        out_ref[s] = rows[s * count : (s + 1) * count]
    for x in range(3 + own_sections):
        for which in range(4):
            copy(x, which).wait_send()


def on_device(u_start, inverses, neighbours, partners):
    count, unknowns = u_start.shape
    devices = lax.axis_size("elem")
    own_sections = SECTIONS // lax.axis_size("section")
    mine = lax.dynamic_slice_in_dim(partners, lax.axis_index("elem") * count, count, 0)
    six = jnp.concatenate([neighbours, mine[:, None]], axis=1)
    exchanges = 3 + own_sections
    column = pltpu.VMEM((unknowns, LANES), jnp.float32)
    vmem = pl.BlockSpec(memory_space=pltpu.VMEM)
    return pl.pallas_call(
        functools.partial(kernel, devices, count),
        out_shape=jax.ShapeDtypeStruct((own_sections, count, unknowns), jnp.float32),
        in_specs=[vmem, vmem, pl.BlockSpec(memory_space=pl.ANY)],
        out_specs=vmem,
        scratch_shapes=[
            pltpu.VMEM((count, unknowns, unknowns), jnp.float32),
            pltpu.VMEM((exchanges, 3 * count, unknowns), jnp.float32),
            pltpu.VMEM((exchanges, 2 * count, LANES), jnp.float32),
            pltpu.VMEM((exchanges, count, LANES), jnp.float32),
            pltpu.VMEM((6, LANES, LANES), jnp.bfloat16),
            pltpu.VMEM((2, 6, FIELDS * FACE, LANES), jnp.float32),
        ]
        + [column] * 10
        + [
            pltpu.VMEM((LANES, unknowns), jnp.float32),
            pltpu.SemaphoreType.DMA((count // GROUP,)),
            pltpu.SemaphoreType.DMA((exchanges, 4)),
            pltpu.SemaphoreType.DMA((exchanges, 4)),
        ],
        compiler_params=pltpu.CompilerParams(
            collective_id=0, has_side_effects=True, vmem_limit_bytes=60 * 1024 * 1024
        ),
    )(u_start, six, inverses)


def solution(mesh):
    placed = (P("elem", None), P("elem", None, None), P("elem", None), P())
    return jax.shard_map(
        on_device, mesh=mesh, in_specs=placed, out_specs=P("section", "elem", None), check_vma=False
    )
```

profile of v0, /device:TPU:0, one launch (start us, length us, event | category | flops | bytes accessed | tf_op | source)
XLA Modules:
  0.0 46.7 jit_solution(2500937901891955779)
XLA Ops:
  0.0 0.0 copy-start
  0.0 0.7 %copy-done = s32[512]{0:T(512)S(1)} copy-done((s32[512]{0:T(512)S(1)}, s32[512]{0:T(512)}, u32[]{:S(2)}) %copy-start) | copy-done | bytes 2072
  0.7 0.1 dynamic-slice_bitcast_fusion
  0.8 0.7 %pad_add_fusion = s32[32,6]{0,1:T(8,128)S(1)} fusion(s32[32,1]{0,1:T(1,128)S(1)} %dynamic-slice_bitcast_fusion, s32[32,5]{0,1:T(8,128)} %param.6), kind=kLoop, calls=%fused_computation | loop fusion | flops 192 | bytes 1536 | tf_op jit(solution)/shard_map/concatenate | solution.py:416
  1.5 0.7 %copy.7.nbr_ref = s32[32,6]{1,0:T(8,128)} copy(s32[32,6]{0,1:T(8,128)S(1)} %pad_add_fusion) | data formatting | bytes 1536 | tf_op jit(solution)/shard_map/concatenate | solution.py:416
  2.1 43.0 %shard_map.46 = f32[2,32,320]{2,1,0:T(8,128)} custom-call(f32[32,320]{1,0:T(8,128)} %u_ref.1, s32[32,6]{1,0:T(8,128)} %copy.7.nbr_ref, f32[32,320,320]{2,1,0:T(8,128)} %inv_ref.1), custom_call_target="tpu_custom_call" | custom-call | tf_op jit(solution)/shard_map/pallas_call | solution.py:420
  45.1 1.5 %copy.9 = f32[2,32,320]{2,1,0:T(8,128)} copy(f32[2,32,320]{2,1,0:T(8,128)} %shard_map.46) | data formatting | bytes 163840
Async XLA Ops:
  0.0 0.7 %copy-start = (s32[512]{0:T(512)S(1)}, s32[512]{0:T(512)}, u32[]{:S(2)}) copy-start(s32[512]{0:T(512)} %param.7) | copy-start | bytes 6148
where the time goes:
time: 46.9 us; the launch traced here: 46.7 us
  Pallas kernels  43 us (92%)
  local copies, waits for them, and re-layouts  2.99 us (6%)
  other arithmetic  0.69 us (1%)
    pallas_call x1, Pallas kernels, on_device(): pl.pallas_call(functools.partial(kernel, devices, count), out_shape=jax.S...  43 us
    unnamed x3, local copies, waits for them, and re-layouts  2.22 us

commit v1 on v0

--- a/solution.py
+++ b/solution.py
@@ -149,8 +149,8 @@
     return out
 
 
-def tendency(uc, uk, faces, out_ref, tk, scale):
-    deriv, inv_weight = lobatto()
+def volume(uc, uk, out_ref, tk, scale):
+    deriv, _ = lobatto()
     for direction in range(3):
         states = [slab(uc, uk, direction, pos) for pos in range(NODE1)]
         speeds = [speed2(state) for state in states]
@@ -162,18 +162,49 @@
                     c = -2.0 * scale * deriv[at][other]
                     terms = [c * x for x in f]
                     sums[at] = terms if sums[at] is None else [x + y for x, y in zip(sums[at], terms)]
-        for upper in range(2):
-            pos = (NODE1 - 1) * upper
-            sign = 2.0 * upper - 1.0
-            other = faces(2 * direction + upper)
-            f = two_point(states[pos], speeds[pos], other, speed2(other), direction)
-            c = -2.0 * scale * inv_weight
-            d = 0.5 * dissipation * c
-            sums[pos] = [
-                total + (c * sign) * x - d * (n - u)
-                for total, x, n, u in zip(sums[pos], f, other, states[pos])
-            ]
         put_slabs(out_ref, tk, direction, sums)
+
+
+def surface(uc, uk, faces, out_ref, tk, scale):
+    _, inv_weight = lobatto()
+
+    def terms(face):
+        direction, upper = face // 2, face % 2
+        own = slab(uc, uk, direction, (NODE1 - 1) * upper)
+        other = faces(face)
+        f = two_point(own, speed2(own), other, speed2(other), direction)
+        c = -2.0 * scale * inv_weight
+        d = 0.5 * dissipation * c
+        sign = 2.0 * upper - 1.0
+        return [(c * sign) * x - d * (n - u) for x, n, u in zip(f, other, own)]
+
+    add_faces(terms, out_ref, tk)
+
+
+def add_faces(terms, out_ref, tk):
+    zero = jnp.zeros((FACE, LANES), jnp.float32)
+    for face in range(6):
+        direction, position = face // 2, (NODE1 - 1) * (face % 2)
+        values = terms(face)
+        for field in range(FIELDS):
+            base = field * NODES
+            rows = slice(base + position * FACE, base + (position + 1) * FACE)
+            there = strided(base + position, FACE)
+            if direction == 0:
+                out_ref[rows, :] = out_ref[rows, :] + values[field]
+            elif direction == 1:
+                tk[there, :] = values[field]
+                if face == 3:
+                    for inner in range(1, NODE1 - 1):
+                        tk[strided(base + inner, FACE), :] = zero
+            else:
+                tk[rows, :] = tk[rows, :] + values[field]
+    for field in range(FIELDS):
+        base = field * NODES
+        for position in range(NODE1):
+            rows = slice(base + position * FACE, base + (position + 1) * FACE)
+            there = strided(base + position, FACE)
+            out_ref[there, :] = out_ref[there, :] + tk[rows, :]
 
 
 def lift(faces, out_ref, tk):
@@ -186,7 +217,7 @@
 
 
 def kernel(
-    devices, count, u_ref, nbr_ref, inv_ref, out_ref,
+    devices, count, u_ref, nbr_ref, partner_ref, inv_ref, out_ref,
     a_ref, recv_ref, zrecv_ref, zsend_ref, pick_ref, near_ref,
     uc, uk, vc, wc, lc, tk, nc, nk, fc, gc, xr,
     a_sem, send_sem, recv_sem,
@@ -215,7 +246,6 @@
     others = (1, -1, rotation, -rotation, rotation + 1, -rotation - 1)
     for offset in others:
         pl.semaphore_signal(barrier, inc=1, device_id={"elem": at(offset)}, device_id_type=MESH)
-    pl.semaphore_wait(barrier, len(others))
 
     def copy(x, which):
         if which < 2:
@@ -231,9 +261,6 @@
             recv_sem=recv_sem.at[x, which], device_id={"elem": target}, device_id_type=MESH,
         )
 
-    copy(0, 0).start()
-    copy(0, 1).start()
-
     def lower_rows(col_ref):
         low = col_ref[strided(0, FIELDS * FACE), :]
         low = jnp.concatenate([low, jnp.zeros((LANES - FIELDS * FACE, LANES), jnp.float32)], axis=0)
@@ -244,8 +271,8 @@
         for s in range(vectors):
             zsend_ref[x + s] = low[s * count : (s + 1) * count]
         for s in range(vectors):
+            copy(x + s, 3).start()
             copy(x + s, 2).start()
-            copy(x + s, 3).start()
         rows = col_ref[...].T
         for s in range(vectors):
             recv_ref[x + s, 2 * count : 3 * count] = rows[s * count : (s + 1) * count]
@@ -254,29 +281,44 @@
             copy(x + s, 1).start()
 
     u_rows = u_ref[...]
-    recv_ref[0, 2 * count : 3 * count] = u_rows
     uc[...] = jnp.concatenate([u_rows] * SECTIONS, axis=0).T
     zsend_ref[0] = lower_rows(uc)[:count]
+    recv_ref[0, 2 * count : 3 * count] = u_rows
+    pl.semaphore_wait(barrier, len(others))
+    copy(0, 3).start()
     copy(0, 2).start()
-    copy(0, 3).start()
+    copy(0, 0).start()
+    copy(0, 1).start()
     to_k_order(uc, uk)
+    volume(uc, uk, lc, tk, 1.0)
 
     lane = lax.broadcasted_iota(jnp.int32, (1, LANES), 1)
     block = lane // count
     local = lane - block * count
+    row = lax.broadcasted_iota(jnp.int32, (LANES, 1), 0)
 
     def ids(*offsets):
-        out = jnp.full((1, LANES), -1, jnp.int32)
+        out = jnp.full((LANES, 1), -1, jnp.int32)
         for index, offset in enumerate(offsets):
-            out = jnp.where(block == index, at(offset) * count + local, out)
+            inside = (row >= index * count) & (row < (index + 1) * count)
+            out = jnp.where(inside, at(offset) * count + row - index * count, out)
         return out
 
     side_ids = ids(-1, 1, 0)
     sliding_ids = ids(rotation, rotation + 1)
+    per_row = LANES // count
+    listed = partner_ref[pl.ds(rank // per_row, 1), :]
+    partner = jnp.zeros((1, LANES), jnp.int32)
+    for index in range(per_row):
+        part_row = jnp.concatenate([listed[:, index * count : (index + 1) * count]] * SECTIONS, axis=1)
+        partner = jnp.where(rank % per_row == index, part_row, partner)
     for face in range(6):
-        match = nbr_ref[:, face : face + 1] == (side_ids if face < 5 else sliding_ids)
-        match = jnp.where(match, 1.0, 0.0)
-        pick_ref[face] = jnp.concatenate([match] * SECTIONS, axis=0).astype(jnp.bfloat16)
+        if face < 5:
+            wanted = jnp.concatenate([nbr_ref[face : face + 1, :]] * SECTIONS, axis=1)
+            match = side_ids == wanted
+        else:
+            match = sliding_ids == partner
+        pick_ref[face] = jnp.where(match, 1.0, 0.0).astype(jnp.bfloat16)
 
     def picked(face, values):
         high = values.astype(jnp.bfloat16)
@@ -285,7 +327,7 @@
         low = (rest - middle.astype(jnp.float32)).astype(jnp.bfloat16)
         split = jnp.concatenate([high, middle, low], axis=0)
         got = lax.dot_general(
-            split, pick_ref[face], (((1,), (1,)), ((), ())), preferred_element_type=jnp.float32
+            split, pick_ref[face], (((1,), (0,)), ((), ())), preferred_element_type=jnp.float32
         )
         n = values.shape[0]
         return (got[2 * n :] + got[n : 2 * n]) + got[:n]
@@ -334,9 +376,8 @@
                 for s in range(vectors)
             ]
 
-            @pl.loop(0, unknowns // ROWS)
-            def _(c):
-                rows = pl.ds(pl.multiple_of(c * ROWS, ROWS), ROWS)
+            for c in range(unknowns // ROWS):
+                rows = slice(c * ROWS, (c + 1) * ROWS)
                 acc = dst[rows, :]
                 for k in range(GROUP):
                     e = g * GROUP + k
@@ -348,7 +389,7 @@
                 dst[rows, :] = acc
 
     receive(0, keep(0))
-    tendency(uc, uk, near(0), lc, tk, 1.0)
+    surface(uc, uk, near(0), lc, tk, 1.0)
     xr[...] = lc[...].T
     matvec(vc, 1, True)
     send(1, vc, 1)
@@ -375,8 +416,9 @@
     def add(face, value):
         near_ref[0, face] = near_ref[0, face] + alphas * near_ref[1, face] + betas * value
 
+    volume(gc, uk, lc, tk, time_step)
     receive(2, add)
-    tendency(gc, uk, near(0), lc, tk, time_step)
+    surface(gc, uk, near(0), lc, tk, time_step)
 
     own_alphas = per_lane(lambda p, g: alpha(own(p, g)))
     own_betas = per_lane(lambda p, g: alpha(own(p, g)) * coupling(own(p, g)))
@@ -388,7 +430,7 @@
         moved = tend if shift == 0 else pltpu.roll(tend, shift * count, 1)
         weights = per_lane(lambda p, g: butcher[own(p, g)][(g - shift) % SECTIONS])
         total = total + weights * moved
-    gc[...] = uc[...] + step
+    gc[...] = step
     xr[...] = total.T
     matvec(fc, own_sections, False)
     send(3, fc, own_sections)
@@ -412,15 +454,14 @@
     count, unknowns = u_start.shape
     devices = lax.axis_size("elem")
     own_sections = SECTIONS // lax.axis_size("section")
-    mine = lax.dynamic_slice_in_dim(partners, lax.axis_index("elem") * count, count, 0)
-    six = jnp.concatenate([neighbours, mine[:, None]], axis=1)
+    listed = partners.reshape(-1, LANES)
     exchanges = 3 + own_sections
     column = pltpu.VMEM((unknowns, LANES), jnp.float32)
     vmem = pl.BlockSpec(memory_space=pltpu.VMEM)
-    return pl.pallas_call(
+    change = pl.pallas_call(
         functools.partial(kernel, devices, count),
         out_shape=jax.ShapeDtypeStruct((own_sections, count, unknowns), jnp.float32),
-        in_specs=[vmem, vmem, pl.BlockSpec(memory_space=pl.ANY)],
+        in_specs=[vmem, vmem, vmem, pl.BlockSpec(memory_space=pl.ANY)],
         out_specs=vmem,
         scratch_shapes=[
             pltpu.VMEM((count, unknowns, unknowns), jnp.float32),
@@ -440,7 +481,8 @@
         compiler_params=pltpu.CompilerParams(
             collective_id=0, has_side_effects=True, vmem_limit_bytes=60 * 1024 * 1024
         ),
-    )(u_start, six, inverses)
+    )(u_start, neighbours.T, listed, inverses)
+    return u_start[None] + change
 
 
 def solution(mesh):

time: 46.9 us -> 40.2 us (0.86)
  Pallas kernels: 43 us -> 38.4 us
  local copies, waits for them, and re-layouts: 2.99 us -> 0.01 us
  other arithmetic: 0.69 us -> 1.54 us
    pallas_call x1, Pallas kernels: 43 us -> 38.4 us  [on_device(): pl.pallas_call(functools.partial(kernel, devices, count), out_shape=jax.S...]
    unnamed x3 -> x2, local copies, waits for them, and re-layouts: 2.22 us -> 0.01 us
    add x0 -> x1, other arithmetic: none -> 1.54 us  [on_device(): return u_start[None] + change]
    concatenate x1 -> x0, other arithmetic: 0.69 us -> none  [on_device(): six = jnp.concatenate([neighbours, mine[:, None]], axis=1)]
    concatenate x1 -> x0, local copies, waits for them, and re-layouts: 0.69 us -> none  [on_device(): six = jnp.concatenate([neighbours, mine[:, None]], axis=1)]
where the time goes in v1:
time: 40.2 us; the launch traced here: 40 us
  Pallas kernels  38.4 us (96%)
  other arithmetic  1.54 us (4%)
    pallas_call x1, Pallas kernels, on_device(): pl.pallas_call(functools.partial(kernel, devices, count), out_shape=jax.S...  38.4 us
    add x1, other arithmetic, on_device(): return u_start[None] + change  1.54 us

profile of v1, /device:TPU:0, one launch (start us, length us, event | category | flops | bytes accessed | tf_op | source)
XLA Modules:
  0.0 40.0 jit_solution(1634888297308374134)
XLA Ops:
  0.0 0.0 copy-start
  0.0 38.4 %shard_map.46 = f32[2,32,320]{2,1,0:T(8,128)} custom-call(f32[32,320]{1,0:T(8,128)} %u_ref.1, s32[5,32]{1,0:T(8,128)} %bitcast.2, s32[4,128]{1,0:T(4,128)} %bitcast.3, f32[32,320,320]{2,1,0:T(8,128)} %inv_ref.1), custom_call_target="tpu_custom_call" | custom-call | tf_op jit(solution)/shard_map/pallas_call | solution.py:461
  38.4 0.0 copy-done
  38.4 1.5 %broadcast_add_fusion = f32[2,32,320]{2,1,0:T(8,128)} fusion(f32[2,32,320]{2,1,0:T(8,128)} %shard_map.46, f32[32,320]{1,0:T(8,128)S(1)} %copy-done), kind=kLoop, calls=%fused_computation | loop fusion | flops 20480 | bytes 204800 | tf_op jit(solution)/shard_map/add | solution.py:485
Async XLA Ops:
  0.0 38.4 %copy-start = (f32[32,320]{1,0:T(8,128)S(1)}, f32[32,320]{1,0:T(8,128)}, u32[]{:S(2)}) copy-start(f32[32,320]{1,0:T(8,128)} %u_ref.1) | copy-start | bytes 122884

commit v2 on v1

--- a/solution.py
+++ b/solution.py
@@ -219,7 +219,7 @@
 def kernel(
     devices, count, u_ref, nbr_ref, partner_ref, inv_ref, out_ref,
     a_ref, recv_ref, zrecv_ref, zsend_ref, pick_ref, near_ref,
-    uc, uk, vc, wc, lc, tk, nc, nk, fc, gc, xr,
+    uc, uk, vc, wc, lc, tk, nc, nk, fc, gc, grp, xr,
     a_sem, send_sem, recv_sem,
 ):
     rank = lax.axis_index("elem")
@@ -247,14 +247,14 @@
     for offset in others:
         pl.semaphore_signal(barrier, inc=1, device_id={"elem": at(offset)}, device_id_type=MESH)
 
-    def copy(x, which):
+    def copy(x, which, start=0, size=count):
         if which < 2:
-            src = u_ref if x == 0 else recv_ref.at[x, pl.ds(2 * count, count)]
-            dst = recv_ref.at[x, pl.ds(which * count, count)]
+            src = u_ref if x == 0 else recv_ref.at[x, pl.ds(2 * count + start, size)]
+            dst = recv_ref.at[x, pl.ds(which * count + start, size)]
             target = at(1) if which == 0 else at(-1)
         else:
-            src = zsend_ref.at[x]
-            dst = zrecv_ref.at[x, pl.ds((which - 2) * count, count)]
+            src = zsend_ref.at[x, pl.ds(start, size)]
+            dst = zrecv_ref.at[x, pl.ds((which - 2) * count + start, size)]
             target = at(-rotation) if which == 2 else at(-rotation - 1)
         return pltpu.make_async_remote_copy(
             src_ref=src, dst_ref=dst, send_sem=send_sem.at[x, which],
@@ -266,19 +266,20 @@
         low = jnp.concatenate([low, jnp.zeros((LANES - FIELDS * FACE, LANES), jnp.float32)], axis=0)
         return low.T
 
-    def send(x, col_ref, vectors):
-        low = lower_rows(col_ref)
-        for s in range(vectors):
-            zsend_ref[x + s] = low[s * count : (s + 1) * count]
-        for s in range(vectors):
-            copy(x + s, 3).start()
-            copy(x + s, 2).start()
-        rows = col_ref[...].T
-        for s in range(vectors):
-            recv_ref[x + s, 2 * count : 3 * count] = rows[s * count : (s + 1) * count]
-        for s in range(vectors):
-            copy(x + s, 0).start()
-            copy(x + s, 1).start()
+    def send(x, vectors, g):
+        start = pl.multiple_of(g * GROUP, GROUP)
+        low = lower_rows(grp)
+        for v in range(vectors):
+            zsend_ref[x + v, pl.ds(start, GROUP)] = low[v * GROUP : (v + 1) * GROUP]
+        for v in range(vectors):
+            copy(x + v, 3, start, GROUP).start()
+            copy(x + v, 2, start, GROUP).start()
+        rows = grp[...].T
+        for v in range(vectors):
+            recv_ref[x + v, pl.ds(2 * count + start, GROUP)] = rows[v * GROUP : (v + 1) * GROUP]
+        for v in range(vectors):
+            copy(x + v, 0, start, GROUP).start()
+            copy(x + v, 1, start, GROUP).start()
 
     u_rows = u_ref[...]
     uc[...] = jnp.concatenate([u_rows] * SECTIONS, axis=0).T
@@ -364,7 +365,10 @@
             out = jnp.where(block == group, value, out)
         return out
 
-    def matvec(dst, vectors, first):
+    cycle = lane % GROUP
+    eighth = lane // GROUP
+
+    def matvec(dst, vectors, first, x=None):
         dst[...] = jnp.zeros_like(dst)
 
         @pl.loop(0, groups)
@@ -372,32 +376,41 @@
             if first:
                 load(g).wait()
             xs = [
-                xr[pl.ds(pl.multiple_of(s * count + g * GROUP, GROUP), GROUP), :]
-                for s in range(vectors)
+                xr[pl.ds(pl.multiple_of(v * count + g * GROUP, GROUP), GROUP), :]
+                for v in range(vectors)
             ]
-
             for c in range(unknowns // ROWS):
                 rows = slice(c * ROWS, (c + 1) * ROWS)
-                acc = dst[rows, :]
+                accs = [jnp.zeros((ROWS, LANES), jnp.float32)] * vectors
                 for k in range(GROUP):
-                    e = g * GROUP + k
-                    a = a_ref[e, rows, :]
-                    for s in range(vectors):
-                        total = jnp.sum(a * xs[s][k : k + 1, :], axis=1, keepdims=True)
-                        where = local == e if vectors == 1 else lane == s * count + e
-                        acc = jnp.where(where, total, acc)
-                dst[rows, :] = acc
+                    a = a_ref[g * GROUP + k, rows, :]
+                    for v in range(vectors):
+                        total = jnp.sum(a * xs[v][k : k + 1, :], axis=1, keepdims=True)
+                        accs[v] = jnp.where(cycle == k, total, accs[v])
+                full = dst[rows, :]
+                for v in range(vectors):
+                    if vectors == 1:
+                        here = local // GROUP == g
+                    else:
+                        here = eighth == v * groups + g
+                    full = jnp.where(here, accs[v], full)
+                dst[rows, :] = full
+                if x is not None:
+                    mine = accs[0]
+                    for v in range(1, vectors):
+                        mine = jnp.where(eighth % vectors == v, accs[v], mine)
+                    grp[rows, :] = mine
+            if x is not None:
+                send(x, vectors, g)
 
     receive(0, keep(0))
     surface(uc, uk, near(0), lc, tk, 1.0)
     xr[...] = lc[...].T
-    matvec(vc, 1, True)
-    send(1, vc, 1)
+    matvec(vc, 1, True, 1)
     receive(1, keep(1))
     lift(near(1), lc, tk)
     xr[...] = lc[...].T
-    matvec(wc, 1, False)
-    send(2, wc, 1)
+    matvec(wc, 1, False, 2)
 
     def alpha(i):
         return time_step * sum(butcher[i])
@@ -432,8 +445,7 @@
         total = total + weights * moved
     gc[...] = step
     xr[...] = total.T
-    matvec(fc, own_sections, False)
-    send(3, fc, own_sections)
+    matvec(fc, own_sections, False, 3)
     receive(3, keep(0))
     for s in range(1, own_sections):
         def merge(face, value, s=s):
@@ -471,7 +483,7 @@
             pltpu.VMEM((6, LANES, LANES), jnp.bfloat16),
             pltpu.VMEM((2, 6, FIELDS * FACE, LANES), jnp.float32),
         ]
-        + [column] * 10
+        + [column] * 11
         + [
             pltpu.VMEM((LANES, unknowns), jnp.float32),
             pltpu.SemaphoreType.DMA((count // GROUP,)),

time: 40.2 us -> 38.9 us (0.968)
  Pallas kernels: 38.4 us -> 37.1 us
    pallas_call x1, Pallas kernels: 38.4 us -> 37.1 us  [on_device(): pl.pallas_call(functools.partial(kernel, devices, count), out_shape=jax.S...]
where the time goes in v2:
time: 38.9 us; the launch traced here: 38.7 us
  Pallas kernels  37.1 us (95%)
  other arithmetic  1.54 us (4%)
    pallas_call x1, Pallas kernels, on_device(): pl.pallas_call(functools.partial(kernel, devices, count), out_shape=jax.S...  37.1 us
    add x1, other arithmetic, on_device(): return u_start[None] + change  1.54 us

profile of v2, /device:TPU:0, one launch (start us, length us, event | category | flops | bytes accessed | tf_op | source)
XLA Modules:
  0.0 38.7 jit_solution(16055582712423606190)
XLA Ops:
  0.0 0.0 copy-start
  0.0 37.1 %shard_map.46 = f32[2,32,320]{2,1,0:T(8,128)} custom-call(f32[32,320]{1,0:T(8,128)} %u_ref.1, s32[5,32]{1,0:T(8,128)} %bitcast.2, s32[4,128]{1,0:T(4,128)} %bitcast.3, f32[32,320,320]{2,1,0:T(8,128)} %inv_ref.1), custom_call_target="tpu_custom_call" | custom-call | tf_op jit(solution)/shard_map/pallas_call | solution.py:473
  37.2 0.0 copy-done
  37.2 1.5 %broadcast_add_fusion = f32[2,32,320]{2,1,0:T(8,128)} fusion(f32[2,32,320]{2,1,0:T(8,128)} %shard_map.46, f32[32,320]{1,0:T(8,128)S(1)} %copy-done), kind=kLoop, calls=%fused_computation | loop fusion | flops 20480 | bytes 204800 | tf_op jit(solution)/shard_map/add | solution.py:497
Async XLA Ops:
  0.0 37.2 %copy-start = (f32[32,320]{1,0:T(8,128)S(1)}, f32[32,320]{1,0:T(8,128)}, u32[]{:S(2)}) copy-start(f32[32,320]{1,0:T(8,128)} %u_ref.1) | copy-start | bytes 122884

commit v3 on v2

--- a/solution.py
+++ b/solution.py
@@ -217,10 +217,11 @@
 
 
 def kernel(
-    devices, count, u_ref, nbr_ref, partner_ref, inv_ref, out_ref,
+    devices, count, u_in, nbr_in, partner_in, inv_ref, out_ref,
+    u_ref, nbr_ref, partner_ref,
     a_ref, recv_ref, zrecv_ref, zsend_ref, pick_ref, near_ref,
     uc, uk, vc, wc, lc, tk, nc, nk, fc, gc, grp, xr,
-    a_sem, send_sem, recv_sem,
+    in_sem, a_sem, send_sem, recv_sem,
 ):
     rank = lax.axis_index("elem")
     part = lax.axis_index("section")
@@ -239,13 +240,20 @@
         block = pl.ds(g * GROUP, GROUP)
         return pltpu.make_async_copy(inv_ref.at[block], a_ref.at[block], a_sem.at[g])
 
-    for g in range(groups):
-        load(g).start()
-
     barrier = pltpu.get_barrier_semaphore()
     others = (1, -1, rotation, -rotation, rotation + 1, -rotation - 1)
     for offset in others:
         pl.semaphore_signal(barrier, inc=1, device_id={"elem": at(offset)}, device_id_type=MESH)
+    small = [
+        pltpu.make_async_copy(src, dst, in_sem.at[index])
+        for index, (src, dst) in enumerate(
+            ((u_in, u_ref), (nbr_in, nbr_ref), (partner_in, partner_ref))
+        )
+    ]
+    for each in small:
+        each.start()
+    for g in range(groups):
+        load(g).start()
 
     def copy(x, which, start=0, size=count):
         if which < 2:
@@ -281,6 +289,8 @@
             copy(x + v, 0, start, GROUP).start()
             copy(x + v, 1, start, GROUP).start()
 
+    for each in small:
+        each.wait()
     u_rows = u_ref[...]
     uc[...] = jnp.concatenate([u_rows] * SECTIONS, axis=0).T
     zsend_ref[0] = lower_rows(uc)[:count]
@@ -473,9 +483,12 @@
     change = pl.pallas_call(
         functools.partial(kernel, devices, count),
         out_shape=jax.ShapeDtypeStruct((own_sections, count, unknowns), jnp.float32),
-        in_specs=[vmem, vmem, vmem, pl.BlockSpec(memory_space=pl.ANY)],
+        in_specs=[pl.BlockSpec(memory_space=pl.ANY)] * 4,
         out_specs=vmem,
         scratch_shapes=[
+            pltpu.VMEM(u_start.shape, jnp.float32),
+            pltpu.VMEM(neighbours.shape[::-1], jnp.int32),
+            pltpu.VMEM(listed.shape, jnp.int32),
             pltpu.VMEM((count, unknowns, unknowns), jnp.float32),
             pltpu.VMEM((exchanges, 3 * count, unknowns), jnp.float32),
             pltpu.VMEM((exchanges, 2 * count, LANES), jnp.float32),
@@ -486,12 +499,13 @@
         + [column] * 11
         + [
             pltpu.VMEM((LANES, unknowns), jnp.float32),
+            pltpu.SemaphoreType.DMA((3,)),
             pltpu.SemaphoreType.DMA((count // GROUP,)),
             pltpu.SemaphoreType.DMA((exchanges, 4)),
             pltpu.SemaphoreType.DMA((exchanges, 4)),
         ],
         compiler_params=pltpu.CompilerParams(
-            collective_id=0, has_side_effects=True, vmem_limit_bytes=60 * 1024 * 1024
+            collective_id=0, has_side_effects=True, vmem_limit_bytes=52 * 1024 * 1024
         ),
     )(u_start, neighbours.T, listed, inverses)
     return u_start[None] + change

time: 38.9 us -> 38.8 us (level)
  local copies, waits for them, and re-layouts: 0.01 us -> 2.17 us
  Pallas kernels: 37.1 us -> 35.8 us
  other arithmetic: 1.54 us -> 0.65 us
    unnamed x2 -> x6, local copies, waits for them, and re-layouts: 0.01 us -> 2.17 us
    pallas_call x1, Pallas kernels: 37.1 us -> 35.8 us  [on_device(): pl.pallas_call(functools.partial(kernel, devices, count), out_shape=jax.S...]
    add x1, other arithmetic: 1.54 us -> 0.65 us  [on_device(): return u_start[None] + change]
where the time goes in v3:
time: 38.8 us; the launch traced here: 38.6 us
  Pallas kernels  35.8 us (92%)
  local copies, waits for them, and re-layouts  2.17 us (6%)
  other arithmetic  0.65 us (2%)
    pallas_call x1, Pallas kernels, on_device(): pl.pallas_call(functools.partial(kernel, devices, count), out_shape=jax.S...  35.8 us
    unnamed x6, local copies, waits for them, and re-layouts  2.17 us

profile of v3, /device:TPU:0, one launch (start us, length us, event | category | flops | bytes accessed | tf_op | source)
XLA Modules:
  0.0 38.6 jit_solution(9222036450082502069)
XLA Ops:
  0.0 0.0 copy-start
  0.0 0.8 %copy-done = f32[32,320]{1,0:T(8,128)S(1)} copy-done((f32[32,320]{1,0:T(8,128)S(1)}, f32[32,320]{1,0:T(8,128)}, u32[]{:S(2)}) %copy-start) | copy-done | bytes 40984
  0.8 0.0 copy-start.1
  0.8 0.7 %copy-done.1 = s32[32,5]{0,1:T(8,128)S(1)} copy-done((s32[32,5]{0,1:T(8,128)S(1)}, s32[32,5]{0,1:T(8,128)}, u32[]{:S(2)}) %copy-start.1) | copy-done | bytes 664
  1.5 0.0 copy-start.2
  1.5 0.7 %copy-done.2 = s32[512]{0:T(512)S(1)} copy-done((s32[512]{0:T(512)S(1)}, s32[512]{0:T(512)}, u32[]{:S(2)}) %copy-start.2) | copy-done | bytes 2072
  2.2 35.8 %shard_map.46 = f32[2,32,320]{2,1,0:T(8,128)S(1)} custom-call(f32[32,320]{1,0:T(8,128)S(1)} %copy-done, s32[5,32]{1,0:T(8,128)S(1)} %bitcast.2, s32[4,128]{1,0:T(4,128)S(1)} %bitcast.3, f32[32,320,320]{2,1,0:T(8,128)} %inv_ref.1), custom_call_target="tpu_custom_call" | custom-call | tf_op jit(solution)/shard_map/pallas_call | solution.py:483
  37.9 0.7 %broadcast_add_fusion = f32[2,32,320]{2,1,0:T(8,128)} fusion(f32[2,32,320]{2,1,0:T(8,128)S(1)} %shard_map.46, f32[32,320]{1,0:T(8,128)S(1)} %copy-done), kind=kLoop, calls=%fused_computation | loop fusion | flops 20480 | bytes 204800 | tf_op jit(solution)/shard_map/add | solution.py:511
Async XLA Ops:
  0.0 0.8 %copy-start = (f32[32,320]{1,0:T(8,128)S(1)}, f32[32,320]{1,0:T(8,128)}, u32[]{:S(2)}) copy-start(f32[32,320]{1,0:T(8,128)} %u_in.1) | copy-start | bytes 122884
  0.8 0.7 %copy-start.1 = (s32[32,5]{0,1:T(8,128)S(1)}, s32[32,5]{0,1:T(8,128)}, u32[]{:S(2)}) copy-start(s32[32,5]{0,1:T(8,128)} %param.6) | copy-start | bytes 1924
  1.5 0.7 %copy-start.2 = (s32[512]{0:T(512)S(1)}, s32[512]{0:T(512)}, u32[]{:S(2)}) copy-start(s32[512]{0:T(512)} %param.7) | copy-start | bytes 6148

commit v4 on v3

--- a/solution.py
+++ b/solution.py
@@ -505,7 +505,7 @@
             pltpu.SemaphoreType.DMA((exchanges, 4)),
         ],
         compiler_params=pltpu.CompilerParams(
-            collective_id=0, has_side_effects=True, vmem_limit_bytes=52 * 1024 * 1024
+            collective_id=0, has_side_effects=True, vmem_limit_bytes=67_043_328
         ),
     )(u_start, neighbours.T, listed, inverses)
     return u_start[None] + change

time: 38.8 us -> 38.3 us (0.987)
  local copies, waits for them, and re-layouts: 2.17 us -> 0 us
  other arithmetic: 0.65 us -> 1.55 us
  Pallas kernels: 35.8 us -> 36.6 us
    unnamed x6 -> x0, local copies, waits for them, and re-layouts: 2.17 us -> none
    add x1, other arithmetic: 0.65 us -> 1.55 us  [on_device(): return u_start[None] + change]
    pallas_call x1, Pallas kernels: 35.8 us -> 36.6 us  [on_device(): pl.pallas_call(functools.partial(kernel, devices, count), out_shape=jax.S...]
where the time goes in v4:
time: 38.3 us; the launch traced here: 38.2 us
  Pallas kernels  36.6 us (96%)
  other arithmetic  1.55 us (4%)
    pallas_call x1, Pallas kernels, on_device(): pl.pallas_call(functools.partial(kernel, devices, count), out_shape=jax.S...  36.6 us
    add x1, other arithmetic, on_device(): return u_start[None] + change  1.55 us

profile of v4, /device:TPU:0, one launch (start us, length us, event | category | flops | bytes accessed | tf_op | source)
XLA Modules:
  0.0 38.2 jit_solution(8514505959155605423)
XLA Ops:
  0.0 36.6 %shard_map.46 = f32[2,32,320]{2,1,0:T(8,128)} custom-call(f32[32,320]{1,0:T(8,128)} %u_in.1, s32[5,32]{1,0:T(8,128)} %bitcast.2, s32[4,128]{1,0:T(4,128)} %bitcast.3, f32[32,320,320]{2,1,0:T(8,128)} %inv_ref.1), custom_call_target="tpu_custom_call" | custom-call | tf_op jit(solution)/shard_map/pallas_call | solution.py:483
  36.6 1.5 %broadcast_add_fusion = f32[2,32,320]{2,1,0:T(8,128)} fusion(f32[2,32,320]{2,1,0:T(8,128)} %shard_map.46, f32[32,320]{1,0:T(8,128)} %u_in.1), kind=kLoop, calls=%fused_computation | loop fusion | flops 20480 | bytes 204800 | tf_op jit(solution)/shard_map/add | solution.py:511

commit v5 on v4

--- a/solution.py
+++ b/solution.py
@@ -85,6 +85,7 @@
 LANES = 128
 GROUP = 8
 ROWS = 64
+MATRIX = 3
 MESH = pl.DeviceIdType.MESH
 
 
@@ -220,7 +221,7 @@
     devices, count, u_in, nbr_in, partner_in, inv_ref, out_ref,
     u_ref, nbr_ref, partner_ref,
     a_ref, recv_ref, zrecv_ref, zsend_ref, pick_ref, near_ref,
-    uc, uk, vc, wc, lc, tk, nc, nk, fc, gc, grp, xr,
+    uc, uk, vc, wc, lc, tk, nc, nk, fc, gc, all_rows, low_rows, half_ref, w_ref, dot_ref, xr,
     in_sem, a_sem, send_sem, recv_sem,
 ):
     rank = lax.axis_index("elem")
@@ -274,17 +275,17 @@
         low = jnp.concatenate([low, jnp.zeros((LANES - FIELDS * FACE, LANES), jnp.float32)], axis=0)
         return low.T
 
-    def send(x, vectors, g):
+    def send(x, vectors, g, dst):
         start = pl.multiple_of(g * GROUP, GROUP)
-        low = lower_rows(grp)
+        low_rows[...] = lower_rows(dst)
+        all_rows[...] = dst[...].T
         for v in range(vectors):
-            zsend_ref[x + v, pl.ds(start, GROUP)] = low[v * GROUP : (v + 1) * GROUP]
+            zsend_ref[x + v, pl.ds(start, GROUP)] = low_rows[pl.ds(v * count + start, GROUP), :]
         for v in range(vectors):
             copy(x + v, 3, start, GROUP).start()
             copy(x + v, 2, start, GROUP).start()
-        rows = grp[...].T
         for v in range(vectors):
-            recv_ref[x + v, pl.ds(2 * count + start, GROUP)] = rows[v * GROUP : (v + 1) * GROUP]
+            recv_ref[x + v, pl.ds(2 * count + start, GROUP)] = all_rows[pl.ds(v * count + start, GROUP), :]
         for v in range(vectors):
             copy(x + v, 0, start, GROUP).start()
             copy(x + v, 1, start, GROUP).start()
@@ -378,13 +379,41 @@
     cycle = lane % GROUP
     eighth = lane // GROUP
 
-    def matvec(dst, vectors, first, x=None):
-        dst[...] = jnp.zeros_like(dst)
-
+    def stacked(high, low, axis):
+        cut = 2 * LANES
+        parts_of = [lax.slice_in_dim(t, 0, cut, axis=axis) for t in (high, low)]
+        parts_of += [lax.slice_in_dim(t, cut, unknowns, axis=axis) for t in (high, low)]
+        return jnp.concatenate(parts_of, axis=axis)
+
+    def halves():
         @pl.loop(0, groups)
         def _(g):
-            if first:
-                load(g).wait()
+            load(g).wait()
+            for k in range(MATRIX):
+                for c in range(unknowns // ROWS):
+                    a = a_ref[g * GROUP + GROUP - MATRIX + k, c * ROWS : (c + 1) * ROWS, :]
+                    high = a.astype(jnp.bfloat16).astype(jnp.float32)
+                    to = k * unknowns + c * ROWS
+                    both = stacked(high, a - high, 1)
+                    half_ref[g, to : to + ROWS, :] = both.astype(jnp.bfloat16)
+
+    def operand(value):
+        xr[...] = value.T
+        high = value.astype(jnp.bfloat16).astype(jnp.float32)
+        low = pltpu.roll(value - high, LANES // 2, 1)
+        both = jnp.where(lane < LANES // 2, high, low)
+        w_ref[...] = stacked(both, both, 0).astype(jnp.bfloat16)
+
+    def matvec(dst, vectors, x=None):
+        dst[...] = jnp.zeros_like(dst)
+        vector_part = GROUP - MATRIX if vectors == 2 else GROUP
+
+        @pl.loop(0, groups)
+        def _(g):
+            if vectors == 2:
+                dot_ref[...] = jnp.dot(
+                    half_ref[g], w_ref[...], preferred_element_type=jnp.float32
+                )
             xs = [
                 xr[pl.ds(pl.multiple_of(v * count + g * GROUP, GROUP), GROUP), :]
                 for v in range(vectors)
@@ -392,7 +421,7 @@
             for c in range(unknowns // ROWS):
                 rows = slice(c * ROWS, (c + 1) * ROWS)
                 accs = [jnp.zeros((ROWS, LANES), jnp.float32)] * vectors
-                for k in range(GROUP):
+                for k in range(vector_part):
                     a = a_ref[g * GROUP + k, rows, :]
                     for v in range(vectors):
                         total = jnp.sum(a * xs[v][k : k + 1, :], axis=1, keepdims=True)
@@ -403,24 +432,31 @@
                         here = local // GROUP == g
                     else:
                         here = eighth == v * groups + g
-                    full = jnp.where(here, accs[v], full)
+                    full = jnp.where(here & (cycle < vector_part), accs[v], full)
                 dst[rows, :] = full
-                if x is not None:
-                    mine = accs[0]
-                    for v in range(1, vectors):
-                        mine = jnp.where(eighth % vectors == v, accs[v], mine)
-                    grp[rows, :] = mine
+            if vectors == 2:
+                for c in range(unknowns // ROWS):
+                    rows = slice(c * ROWS, (c + 1) * ROWS)
+                    got = dot_ref[rows, :]
+                    for k in range(1, MATRIX):
+                        more = dot_ref[k * unknowns + c * ROWS : k * unknowns + (c + 1) * ROWS, :]
+                        got = jnp.where(cycle == vector_part + k, more, got)
+                    got = got + pltpu.roll(got, LANES // 2, 1)
+                    here = (block < 2) & (local // GROUP == g) & (cycle >= vector_part)
+                    dst[rows, :] = jnp.where(here, got, dst[rows, :])
             if x is not None:
-                send(x, vectors, g)
+                send(x, vectors, g, dst)
+
+    halves()
 
     receive(0, keep(0))
     surface(uc, uk, near(0), lc, tk, 1.0)
     xr[...] = lc[...].T
-    matvec(vc, 1, True, 1)
+    matvec(vc, 1, 1)
     receive(1, keep(1))
     lift(near(1), lc, tk)
     xr[...] = lc[...].T
-    matvec(wc, 1, False, 2)
+    matvec(wc, 1, 2)
 
     def alpha(i):
         return time_step * sum(butcher[i])
@@ -454,16 +490,16 @@
         weights = per_lane(lambda p, g: butcher[own(p, g)][(g - shift) % SECTIONS])
         total = total + weights * moved
     gc[...] = step
-    xr[...] = total.T
-    matvec(fc, own_sections, False, 3)
+    operand(total)
+    matvec(fc, own_sections, 3)
     receive(3, keep(0))
     for s in range(1, own_sections):
         def merge(face, value, s=s):
             near_ref[0, face] = jnp.where(block == s, value, near_ref[0, face])
         receive(3 + s, merge)
     lift(near(0), lc, tk)
-    xr[...] = (own_couplings * lc[...]).T
-    matvec(wc, own_sections, False)
+    operand(own_couplings * lc[...])
+    matvec(wc, own_sections)
     rows = (gc[...] + fc[...] + wc[...]).T
     for s in range(own_sections):
         out_ref[s] = rows[s * count : (s + 1) * count]
@@ -496,8 +532,13 @@
             pltpu.VMEM((6, LANES, LANES), jnp.bfloat16),
             pltpu.VMEM((2, 6, FIELDS * FACE, LANES), jnp.float32),
         ]
-        + [column] * 11
+        + [column] * 10
         + [
+            pltpu.VMEM((LANES, unknowns), jnp.float32),
+            pltpu.VMEM((LANES, LANES), jnp.float32),
+            pltpu.VMEM((count // GROUP, MATRIX * unknowns, 2 * unknowns), jnp.bfloat16),
+            pltpu.VMEM((2 * unknowns, LANES), jnp.bfloat16),
+            pltpu.VMEM((MATRIX * unknowns, LANES), jnp.float32),
             pltpu.VMEM((LANES, unknowns), jnp.float32),
             pltpu.SemaphoreType.DMA((3,)),
             pltpu.SemaphoreType.DMA((count // GROUP,)),

time: 38.3 us -> 38 us (level)
  no operation moved by 1% of the time
where the time goes in v5:
time: 38 us; the launch traced here: 37.8 us
  Pallas kernels  36.3 us (96%)
  other arithmetic  1.55 us (4%)
    pallas_call x1, Pallas kernels, on_device(): pl.pallas_call(functools.partial(kernel, devices, count), out_shape=jax.S...  36.3 us
    add x1, other arithmetic, on_device(): return u_start[None] + change  1.55 us

profile of v5, /device:TPU:0, one launch (start us, length us, event | category | flops | bytes accessed | tf_op | source)
XLA Modules:
  0.0 37.8 jit_solution(12278087827054668812)
XLA Ops:
  0.0 36.3 %shard_map.46 = f32[2,32,320]{2,1,0:T(8,128)} custom-call(f32[32,320]{1,0:T(8,128)} %u_in.1, s32[5,32]{1,0:T(8,128)} %bitcast.2, s32[4,128]{1,0:T(4,128)} %bitcast.3, f32[32,320,320]{2,1,0:T(8,128)} %inv_ref.1), custom_call_target="tpu_custom_call" | custom-call | tf_op jit(solution)/shard_map/pallas_call | solution.py:519
  36.3 1.5 %broadcast_add_fusion = f32[2,32,320]{2,1,0:T(8,128)} fusion(f32[2,32,320]{2,1,0:T(8,128)} %shard_map.46, f32[32,320]{1,0:T(8,128)} %u_in.1), kind=kLoop, calls=%fused_computation | loop fusion | flops 20480 | bytes 204800 | tf_op jit(solution)/shard_map/add | solution.py:552
